TPU v7x, 512 devices: a whole 4x4x16 slice. The times are simulated.
512 devices in a mesh: dp: 64 (over z, x_lo, core), seq: 8 (over x_hi, y).
Axes of the slice: x: 4 (x_hi: 2, x_lo: 2; x = x_hi * 2 + x_lo), y: 4, z: 16, core: 2. Of those that a mesh axis runs over, the one named last changes fastest.
Arguments:
- queries: bfloat16 [65536, 3072], P(('dp', 'seq')), may hold values from -6 to 6
- key_states: bfloat16 [65536, 3072], P(('dp', 'seq')), may hold values from -6 to 6
- value_states: bfloat16 [65536, 3072], P(('dp', 'seq')), may hold values from -6 to 6
- grad_out: bfloat16 [65536, 2560], P(('dp', 'seq')), may hold values from -24 to 24
- out_weight: bfloat16 [3072, 2560], P('seq', 'dp'), may hold values from -0.109375 to 0.109375
- key_blocks: int32 [24, 16, 16], replicated, may hold values from 0 to 15, as said below
- key_count: int32 [24, 16], replicated, may hold values from 5 to 16
Outputs:
- grad_queries: bfloat16 [65536, 3072], P(('dp', 'seq'))
- grad_keys: bfloat16 [65536, 3072], P(('dp', 'seq'))
- grad_weight: float32 [3072, 2560], P('seq', 'dp')
Inputs may be any that keep to these rules, and one draw needn't show every extreme that they name: The first key_count[h, b] entries of key_blocks[h, b] name distinct key blocks; later entries name the other blocks and are not used. Query blocks 0 and 15 attend all 16 blocks; every other query block attends at most 8 blocks, and some reach 8 for every head.
All inputs are finite; a program needn't handle non-finite values.
Results may differ from a plain program's by a relative error of at most 0.0079.
Values may be sent and summed in bfloat16 or wider, within the bound.
A program may use at most 64 MiB of HBM per device.

v0:
```python
import jax
import jax.numpy as jnp
from jax import lax
from jax.sharding import PartitionSpec as P

HEADS = 24
HD = 128
BLK = 64
RANDB = 3


def forward_rows(query_rows, key_rows, value_rows, live_keys):
    scores = jnp.einsum(
        "rqd,rkd->rqk", query_rows, key_rows, preferred_element_type=jnp.float32
    ) * HD ** (-0.5)
    if live_keys is not None:
        scores = jnp.where(live_keys[:, None, :], scores, -jnp.inf)
    row_max = jnp.max(scores, axis=-1, keepdims=True)
    expo = jnp.exp(scores - row_max)
    probs = expo / jnp.sum(expo, axis=-1, keepdims=True)
    head_out = jnp.einsum(
        "rqk,rkd->rqd", probs.astype(jnp.bfloat16), value_rows, preferred_element_type=jnp.float32
    )
    return (probs, head_out.astype(jnp.bfloat16))


def backward_rows(query_rows, key_rows, value_rows, grad_rows, probs):
    dprob = jnp.einsum("rqd,rkd->rqk", grad_rows, value_rows, preferred_element_type=jnp.float32)
    row_delta = jnp.sum(probs * dprob, axis=-1, keepdims=True)
    dscore = (probs * (dprob - row_delta) * HD ** (-0.5)).astype(jnp.bfloat16)
    grad_q = jnp.einsum("rqk,rkd->rqd", dscore, key_rows, preferred_element_type=jnp.float32)
    grad_k = jnp.einsum("rqk,rqd->rkd", dscore, query_rows, preferred_element_type=jnp.float32)
    return (grad_q, grad_k)


def arrange(head_item):
    query_head, key_head, value_head, grad_head, block_list, block_count = head_item
    seq_length = query_head.shape[0]
    block_total = seq_length // BLK
    slot_count = min(block_total, 5 + RANDB)
    middle = block_total - 2
    query_blocks = query_head.reshape(block_total, BLK, HD)
    key_blocks_here = key_head.reshape(block_total, BLK, HD)
    value_blocks = value_head.reshape(block_total, BLK, HD)
    grad_blocks = grad_head.reshape(block_total, BLK, HD)
    chosen = block_list[1 : block_total - 1, :slot_count]
    live_keys = jnp.repeat(
        jnp.arange(slot_count)[None, :] < block_count[1 : block_total - 1, None], BLK, axis=1
    )
    mid_keys = key_blocks_here[chosen].reshape(middle, slot_count * BLK, HD)
    mid_values = value_blocks[chosen].reshape(middle, slot_count * BLK, HD)
    middle_group = (
        query_blocks[1 : block_total - 1],
        mid_keys,
        mid_values,
        grad_blocks[1 : block_total - 1],
        live_keys,
    )
    edge_queries = jnp.stack((query_blocks[0], query_blocks[block_total - 1]))
    edge_grads = jnp.stack((grad_blocks[0], grad_blocks[block_total - 1]))
    edge_keys = jnp.broadcast_to(key_head[None], (2, seq_length, HD))
    edge_values = jnp.broadcast_to(value_head[None], (2, seq_length, HD))
    edge_group = (edge_queries, edge_keys, edge_values, edge_grads, None)
    return (middle_group, edge_group, chosen)


def join_rows(edge_part, middle_part):
    return jnp.concatenate((edge_part[:1], middle_part, edge_part[1:]), axis=0).reshape(-1, HD)


def attend_full(head_item):
    middle_group, edge_group, chosen = arrange(head_item)
    mid_probs, mid_out = forward_rows(
        middle_group[0], middle_group[1], middle_group[2], middle_group[4]
    )
    edge_probs, edge_out = forward_rows(edge_group[0], edge_group[1], edge_group[2], None)
    mid_dq, mid_dk = backward_rows(
        middle_group[0], middle_group[1], middle_group[2], middle_group[3], mid_probs
    )
    edge_dq, edge_dk = backward_rows(
        edge_group[0], edge_group[1], edge_group[2], edge_group[3], edge_probs
    )
    block_total = head_item[0].shape[0] // BLK
    slot_count = chosen.shape[1]
    spread = (chosen[:, :, None] == jnp.arange(block_total)[None, None, :]).astype(jnp.float32)
    key_sum = jnp.einsum(
        "msn,msbd->nbd",
        spread,
        mid_dk.reshape(chosen.shape[0], slot_count, BLK, HD),
        precision=lax.Precision.HIGHEST,
    ).reshape(-1, HD)
    key_sum = key_sum + jnp.sum(edge_dk, axis=0)
    grad_query = join_rows(edge_dq, mid_dq).astype(jnp.bfloat16)
    return (join_rows(edge_out, mid_out), grad_query, key_sum.astype(jnp.bfloat16))


def project_back(whole_grad, out_weight):
    whole_rows = lax.all_gather(out_weight, "dp", axis=1, tiled=True)
    return lax.dot_general(
        whole_grad, whole_rows, (((1,), (1,)), ((), ())), preferred_element_type=jnp.float32
    )


def reduce_grads(head_outputs, whole_grad):
    local_count = head_outputs.shape[0]
    local_sum = jnp.einsum(
        "hld,lc->hdc", head_outputs, whole_grad, preferred_element_type=jnp.float32
    )
    local_sum = local_sum.reshape(local_count * HD, whole_grad.shape[1])
    return lax.psum_scatter(local_sum, "dp", scatter_dimension=1, tiled=True)


def per_device(queries, key_states, value_states, grad_out, out_weight, key_blocks, key_count):
    group_size = lax.axis_size("seq")
    local_heads = HEADS // group_size
    query_all, key_all, value_all = (
        lax.all_to_all(queries, "seq", split_axis=1, concat_axis=0, tiled=True),
        lax.all_to_all(key_states, "seq", split_axis=1, concat_axis=0, tiled=True),
        lax.all_to_all(value_states, "seq", split_axis=1, concat_axis=0, tiled=True),
    )
    whole_grad = lax.all_gather(grad_out, "seq", axis=0, tiled=True)
    seq_length = query_all.shape[0]
    first_head = lax.axis_index("seq") * local_heads
    lists_here = lax.dynamic_slice_in_dim(key_blocks, first_head, local_heads, 0)
    counts_here = lax.dynamic_slice_in_dim(key_count, first_head, local_heads, 0)
    grad_heads = project_back(whole_grad, out_weight).astype(jnp.bfloat16)

    def split_heads(array_in):
        return array_in.reshape(seq_length, local_heads, HD).transpose(1, 0, 2)

    def merge_heads(array_in):
        return array_in.transpose(1, 0, 2).reshape(seq_length, local_heads * HD)

    stacked = (
        split_heads(query_all),
        split_heads(key_all),
        split_heads(value_all),
        split_heads(grad_heads),
        lists_here,
        counts_here,
    )
    head_outputs, grad_q, grad_k = lax.map(attend_full, stacked)
    weight_part = reduce_grads(head_outputs, whole_grad)
    grad_queries, grad_keys = (
        lax.all_to_all(merge_heads(grad_q), "seq", split_axis=0, concat_axis=1, tiled=True),
        lax.all_to_all(merge_heads(grad_k), "seq", split_axis=0, concat_axis=1, tiled=True),
    )
    return (grad_queries, grad_keys, weight_part)


def solution(mesh):
    return jax.shard_map(
        per_device,
        mesh=mesh,
        in_specs=(
            P(("dp", "seq"), None),
            P(("dp", "seq"), None),
            P(("dp", "seq"), None),
            P(("dp", "seq"), None),
            P("seq", "dp"),
            P(),
            P(),
        ),
        out_specs=(P(("dp", "seq"), None), P(("dp", "seq"), None), P("seq", "dp")),
        check_vma=False,
    )
```

profile of v0, /device:TPU:8, one launch (start us, length us, event | category | flops | bytes accessed | tf_op | source)
XLA Modules:
  0.0 640.3 jit_solution(14986661294399659930)
XLA Ops:
  8.7 2.3 copy.56
  11.0 9.3 %all-to-all-start = ((bf16[128,8,384]{0,2,1:T(8,128)(2,1)}), bf16[128,8,384]{0,2,1:T(8,128)(2,1)S(1)}, u32[]{:S(2)}, u32[]{:S(2)}) async-start(bf16[128,8,384]{0,2,1:T(8,128)(2,1)} %bitcast.19), calls=%async_computation | async-start | bytes 1572864 | tf_op jit(solution)/shard_map/all_to_all | solution.py:117
  21.4 8.7 %all-to-all-done = bf16[128,8,384]{0,2,1:T(8,128)(2,1)S(1)} async-done(((bf16[128,8,384]{0,2,1:T(8,128)(2,1)}), bf16[128,8,384]{0,2,1:T(8,128)(2,1)S(1)}, u32[]{:S(2)}, u32[]{:S(2)}) %all-to-all-start) | async-done | bytes 786464 | tf_op jit(solution)/shard_map/all_to_all | solution.py:117
  30.1 5.4 all-to-all-start.1
  35.5 1.2 copy.60
  36.6 11.0 %all-to-all-done.1 = bf16[128,8,384]{0,2,1:T(8,128)(2,1)S(1)} async-done(((bf16[128,8,384]{0,2,1:T(8,128)(2,1)}), bf16[128,8,384]{0,2,1:T(8,128)(2,1)S(1)}, u32[]{:S(2)}, u32[]{:S(2)}) %all-to-all-start.1) | async-done | bytes 786464 | tf_op jit(solution)/shard_map/all_to_all | solution.py:118
  47.6 4.9 all-to-all-start.2
  54.9 1.3 reshape.100
  56.2 8.3 %all-to-all-done.2 = bf16[128,8,384]{0,2,1:T(8,128)(2,1)S(1)} async-done(((bf16[128,8,384]{0,2,1:T(8,128)(2,1)}), bf16[128,8,384]{0,2,1:T(8,128)(2,1)S(1)}, u32[]{:S(2)}, u32[]{:S(2)}) %all-to-all-start.2) | async-done | bytes 786464 | tf_op jit(solution)/shard_map/all_to_all | solution.py:119
  65.0 1.2 reshape.101
  66.2 70.3 %all-gather.5.cloned.1.call-done = bf16[384,2560]{0,1:T(8,128)(2,1)} async-done(((bf16[384,40]{0,1:T(8,128)(2,1)}), bf16[384,2560]{0,1:T(8,128)(2,1)}) %all-gather.5.cloned.1.call-update) | async-done | bytes 1966096 | tf_op jit(solution)/shard_map/all_gather | solution.py:98
  136.6 93.7 %all-gather.3.cloned.1.call-done = bf16[1024,2560]{1,0:T(8,128)(2,1)} async-done(((bf16[128,2560]{1,0:T(8,128)(2,1)}), bf16[1024,2560]{1,0:T(8,128)(2,1)}) %all-gather.3.cloned.1.call-update) | async-done | bytes 5242896 | tf_op jit(solution)/shard_map/all_gather | solution.py:121
  230.3 5.3 convolution_convert_fusion.3
  235.7 1.2 copy.64
  236.8 152.2 %while.14 = (s32[]{:T(128)}, bf16[3,1024,128]{2,1,0:T(8,128)(2,1)}, bf16[3,1024,128]{2,1,0:T(8,128)(2,1)}, bf16[3,1024,128]{2,1,0:T(8,128)(2,1)}, bf16[3,1024,12...) while((s32[]{:T(128)}, bf16[3,1024,128]{2,1,0:T(8,128)(2,1)}, ...), condition=%wide.region_7.8_spmd, body=%wide.region_0.7_spmd.sunk | while | flops 979120320 | bytes 70489952 | solution.py:142
  246.1 2.1 gather_fusion.1
  248.2 3.5 fusion.160
  252.5 1.8 fusion.162
  254.3 3.7 convolution_convert_fusion.9
  258.0 8.7 %fusion.163 = bf16[14,64,128]{2,1,0:T(8,128)(2,1)} fusion(bf16[14,512,128]{2,1,0:T(8,128)(2,1)S(1)} %bitcast.145, f32[14,64,512]{2,1,0:T(8,128)} %fusion.160, f32[14,64,512]{2,1,0:T(8,128)} %get-tuple-element.217, f32[14,64]{1,0:T(8,128)S(1)} %get-tuple-element.218), kind=kOutput, calls=%fused_computation.27.clone.1 | convolution fusion | flops 120767872 | bytes 5737984 | tf_op jit(solution)/shard_map/while/body/eval_jaxpr/rqk,rkd->rqd/dot_general | solution.py:31
  266.7 10.8 %fusion.165 = f32[14,512,128]{2,1,0:T(8,128)} fusion(bf16[14,64,128]{2,1,0:T(8,128)(2,1)S(1)} %bitcast.152, f32[14,64,512]{2,1,0:T(8,128)} %fusion.160, f32[14,64,512]{2,1,0:T(8,128)} %get-tuple-element.217, f32[14,64]{1,0:T(8,128)S(1)} %get-tuple-element.218), kind=kOutput, calls=%fused_computation.14.clone.1 | convolution fusion | flops 120653184 | bytes 7572992 | tf_op jit(solution)/shard_map/while/body/eval_jaxpr/rqk,rqd->rkd/dot_general | solution.py:32
  277.5 6.1 fusion.166
  283.8 2.4 fusion.167
  296.8 2.1 gather_fusion.1
  298.9 3.5 fusion.160
  303.2 1.8 fusion.162
  305.0 3.7 convolution_convert_fusion.9
  308.7 8.7 %fusion.163 = bf16[14,64,128]{2,1,0:T(8,128)(2,1)} fusion(bf16[14,512,128]{2,1,0:T(8,128)(2,1)S(1)} %bitcast.145, f32[14,64,512]{2,1,0:T(8,128)} %fusion.160, f32[14,64,512]{2,1,0:T(8,128)} %get-tuple-element.217, f32[14,64]{1,0:T(8,128)S(1)} %get-tuple-element.218), kind=kOutput, calls=%fused_computation.27.clone.1 | convolution fusion | flops 120767872 | bytes 5737984 | tf_op jit(solution)/shard_map/while/body/eval_jaxpr/rqk,rkd->rqd/dot_general | solution.py:31
  317.4 10.8 %fusion.165 = f32[14,512,128]{2,1,0:T(8,128)} fusion(bf16[14,64,128]{2,1,0:T(8,128)(2,1)S(1)} %bitcast.152, f32[14,64,512]{2,1,0:T(8,128)} %fusion.160, f32[14,64,512]{2,1,0:T(8,128)} %get-tuple-element.217, f32[14,64]{1,0:T(8,128)S(1)} %get-tuple-element.218), kind=kOutput, calls=%fused_computation.14.clone.1 | convolution fusion | flops 120653184 | bytes 7572992 | tf_op jit(solution)/shard_map/while/body/eval_jaxpr/rqk,rqd->rkd/dot_general | solution.py:32
  328.2 6.1 fusion.166
  334.5 2.5 fusion.167
  347.6 2.1 gather_fusion.1
  349.7 3.5 fusion.160
  353.9 1.8 fusion.162
  355.7 3.7 convolution_convert_fusion.9
  359.5 8.7 %fusion.163 = bf16[14,64,128]{2,1,0:T(8,128)(2,1)} fusion(bf16[14,512,128]{2,1,0:T(8,128)(2,1)S(1)} %bitcast.145, f32[14,64,512]{2,1,0:T(8,128)} %fusion.160, f32[14,64,512]{2,1,0:T(8,128)} %get-tuple-element.217, f32[14,64]{1,0:T(8,128)S(1)} %get-tuple-element.218), kind=kOutput, calls=%fused_computation.27.clone.1 | convolution fusion | flops 120767872 | bytes 5737984 | tf_op jit(solution)/shard_map/while/body/eval_jaxpr/rqk,rkd->rqd/dot_general | solution.py:31
  368.2 10.8 %fusion.165 = f32[14,512,128]{2,1,0:T(8,128)} fusion(bf16[14,64,128]{2,1,0:T(8,128)(2,1)S(1)} %bitcast.152, f32[14,64,512]{2,1,0:T(8,128)} %fusion.160, f32[14,64,512]{2,1,0:T(8,128)} %get-tuple-element.217, f32[14,64]{1,0:T(8,128)S(1)} %get-tuple-element.218), kind=kOutput, calls=%fused_computation.14.clone.1 | convolution fusion | flops 120653184 | bytes 7572992 | tf_op jit(solution)/shard_map/while/body/eval_jaxpr/rqk,rqd->rkd/dot_general | solution.py:32
  379.0 6.1 fusion.166
  385.3 2.4 fusion.167
  389.0 6.9 %fusion.81 = f32[3,128,2560]{2,1,0:T(8,128)} fusion(bf16[3,1024,128]{2,1,0:T(8,128)(2,1)} %get-tuple-element.59, bf16[1024,2560]{1,0:T(8,128)(2,1)} %all-gather.3.cloned.1.call-done), kind=kOutput, calls=%fused_computation.93 | convolution fusion | flops 2013265920 | bytes 9961472 | tf_op jit(solution)/shard_map/hld,lc->hdc/dot_general | solution.py:106
  395.9 5.6 copy.73
  404.1 5.2 all-to-all-start.4
  410.8 10.5 %all-to-all-done.4 = bf16[8,128,384]{1,2,0:T(8,128)(2,1)S(1)} async-done(((bf16[8,128,384]{1,2,0:T(8,128)(2,1)}), bf16[8,128,384]{1,2,0:T(8,128)(2,1)S(1)}, u32[]{:S(2)}, u32[]{:S(2)}) %all-to-all-start.4) | async-done | bytes 786464 | tf_op jit(solution)/shard_map/all_to_all | solution.py:146
  421.3 5.1 all-to-all-start.3
  426.3 1.2 copy.75
  427.5 12.9 %all-to-all-done.3 = bf16[8,128,384]{1,2,0:T(8,128)(2,1)S(1)} async-done(((bf16[8,128,384]{1,2,0:T(8,128)(2,1)}), bf16[8,128,384]{1,2,0:T(8,128)(2,1)S(1)}, u32[]{:S(2)}, u32[]{:S(2)}) %all-to-all-start.3) | async-done | bytes 786464 | tf_op jit(solution)/shard_map/all_to_all | solution.py:145
  440.4 1.2 copy.74
  441.5 192.2 %reduce-scatter.5.cloned.1.call-done = f32[384,40]{0,1:T(8,128)} async-done(((f32[384,2560]{0,1:T(8,128)}), f32[384,40]{0,1:T(8,128)}) %reduce-scatter.5.cloned.1.call-update) | async-done | bytes 61456
  (201 shorter events, 43.6 us)
Async XLA Ops:
  7.2 45.5 %copy-start = (s32[24,16,16]{0,2,1:T(8,128)S(1)}, s32[24,16,16]{0,2,1:T(8,128)}, u32[]{:S(2)}) copy-start(s32[24,16,16]{0,2,1:T(8,128)} %param.14) | copy-start | bytes 73732
  7.2 129.4 %all-gather.5.cloned.1.call-start = ((), (), s32[]{:S(2)}) async-start(), calls=%async_computation.7 | async-start | bytes 1996800 | tf_op jit(solution)/shard_map/all_gather | solution.py:98
  7.9 12.3 %copy-start.8 = (bf16[128,3072]{1,0:T(8,128)(2,1)S(1)}, bf16[128,3072]{1,0:T(8,128)(2,1)}, u32[]{:S(2)}) copy-start(bf16[128,3072]{1,0:T(8,128)(2,1)} %param.10) | copy-start | bytes 2359300
  7.9 222.4 %all-gather.3.cloned.1.call-start = ((), (), s32[]{:S(2)}) async-start(), calls=%async_computation.6 | async-start | bytes 5898240 | tf_op jit(solution)/shard_map/all_gather | solution.py:121
  11.0 19.1 %all-to-all-start = ((bf16[128,8,384]{0,2,1:T(8,128)(2,1)}), bf16[128,8,384]{0,2,1:T(8,128)(2,1)S(1)}, u32[]{:S(2)}, u32[]{:S(2)}) async-start(bf16[128,8,384]{0,2,1:T(8,128)(2,1)} %bitcast.19), calls=%async_computation | async-start | bytes 1572864 | tf_op jit(solution)/shard_map/all_to_all | solution.py:117
  20.2 15.2 %copy-start.9 = (bf16[128,3072]{1,0:T(8,128)(2,1)S(1)}, bf16[128,3072]{1,0:T(8,128)(2,1)}, u32[]{:S(2)}) copy-start(bf16[128,3072]{1,0:T(8,128)(2,1)} %param.11) | copy-start | bytes 2359300
  30.1 17.5 %all-to-all-start.1 = ((bf16[128,8,384]{0,2,1:T(8,128)(2,1)}), bf16[128,8,384]{0,2,1:T(8,128)(2,1)S(1)}, u32[]{:S(2)}, u32[]{:S(2)}) async-start(bf16[128,8,384]{0,2,1:T(8,128)(2,1)} %bitcast.22), calls=%async_computation.1 | async-start | bytes 1572864 | tf_op jit(solution)/shard_map/all_to_all | solution.py:118
  35.5 17.0 %copy-start.14 = (s32[24,16]{0,1:T(8,128)S(1)}, s32[24,16]{0,1:T(8,128)}, u32[]{:S(2)}) copy-start(s32[24,16]{0,1:T(8,128)} %param.15) | copy-start | bytes 4612
  47.6 16.9 %all-to-all-start.2 = ((bf16[128,8,384]{0,2,1:T(8,128)(2,1)}), bf16[128,8,384]{0,2,1:T(8,128)(2,1)S(1)}, u32[]{:S(2)}, u32[]{:S(2)}) async-start(bf16[128,8,384]{0,2,1:T(8,128)(2,1)} %bitcast.25), calls=%async_computation.2 | async-start | bytes 1572864 | tf_op jit(solution)/shard_map/all_to_all | solution.py:119
  52.5 581.3 %reduce-scatter.5.cloned.1.call-start = ((), (), s32[]{:S(2)}) async-start(), calls=%async_computation.8 | async-start | bytes 3993600
  236.8 2.1 copy-start.15
  236.9 3.6 copy-start.3
  243.1 0.9 copy-start.2
  243.6 1.0 copy-start.12
  252.5 1.8 copy-start.1
  277.5 6.3 copy-start.13
  283.6 2.7 copy-start.5
  283.8 2.5 copy-start.6
  283.8 2.5 copy-start.7
  286.3 1.3 copy-start.4
  286.3 1.3 copy-start.16
  287.6 2.1 copy-start.15
  287.6 3.6 copy-start.3
  293.8 0.9 copy-start.2
  294.3 1.0 copy-start.12
  303.2 1.8 copy-start.1
  328.2 6.3 copy-start.13
  334.3 2.7 copy-start.5
  334.5 2.6 copy-start.6
  334.5 2.6 copy-start.7
  337.0 1.3 copy-start.4
  337.0 1.3 copy-start.16
  338.3 2.1 copy-start.15
  338.3 3.6 copy-start.3
  344.5 0.9 copy-start.2
  345.0 1.0 copy-start.12
  353.9 1.8 copy-start.1
  379.0 6.3 copy-start.13
  385.1 2.7 copy-start.5
  385.2 2.5 copy-start.6
  385.3 2.5 copy-start.7
  387.7 1.3 copy-start.4
  387.7 1.3 copy-start.16
  401.5 1.1 copy-start.10
  403.1 6.2 copy-start.11
  404.1 17.2 %all-to-all-start.4 = ((bf16[8,128,384]{1,2,0:T(8,128)(2,1)}), bf16[8,128,384]{1,2,0:T(8,128)(2,1)S(1)}, u32[]{:S(2)}, u32[]{:S(2)}) async-start(bf16[8,128,384]{1,2,0:T(8,128)(2,1)} %copy.71), calls=%async_computation.4 | async-start | bytes 1572864 | tf_op jit(solution)/shard_map/all_to_all | solution.py:146
  421.3 19.1 %all-to-all-start.3 = ((bf16[8,128,384]{1,2,0:T(8,128)(2,1)}), bf16[8,128,384]{1,2,0:T(8,128)(2,1)S(1)}, u32[]{:S(2)}, u32[]{:S(2)}) async-start(bf16[8,128,384]{1,2,0:T(8,128)(2,1)} %copy.69), calls=%async_computation.3 | async-start | bytes 1572864 | tf_op jit(solution)/shard_map/all_to_all | solution.py:145
Sparse Core Ops, SparseCore 0:
  10.2 126.3 all-gather.4
  139.7 90.5 all-gather.2
  401.6 232.0 reduce-scatter.4
where the time goes:
time: 642 us; the launch traced here: 640 us
  waiting for transfers between devices  409 us (64%)
  matrix products  126 us (20%)
  local copies, waits for them, and re-layouts  55.3 us (9%)
  starting transfers between devices  29.9 us (5%)
  between operations  13.9 us (2%)
    unnamed x4, waiting for transfers between devices  194 us
    all_gather x1, waiting for transfers between devices, per_device(): whole_grad = lax.all_gather(grad_out, 'seq', axis=0, tiled=True)  93.7 us
    all_gather x1, waiting for transfers between devices, project_back(): whole_rows = lax.all_gather(out_weight, 'dp', axis=1, tiled=True)  70.3 us
    dot_general x6, matrix products, backward_rows(): jnp.einsum('rqk,rqd->rkd', dscore, query_rows, preferred_element_type=jnp...  39.7 us
    dot_general x6, matrix products, backward_rows(): jnp.einsum('rqk,rkd->rqd', dscore, key_rows, preferred_element_type=jnp.f...  27.4 us
    dot_general x3, matrix products, attend_full(): jnp.einsum('msn,msbd->nbd', spread, mid_dk.reshape(chosen.shape[0], slot_...  18.3 us
    dot_general x6, matrix products, forward_rows(): jnp.einsum('rqk,rkd->rqd', probs.astype(jnp.bfloat16), value_rows, prefer...  12.9 us
    all_to_all x1, waiting for transfers between devices, per_device(): lax.all_to_all(merge_heads(grad_q), 'seq', split_axis=0, concat_axis=1, t...  12.9 us
  transfers between devices with their start and end apart: 8, of which 8 were waited for; matrix products, arithmetic and copies ran while one was open for 2% of the time, Pallas kernels for 0%

commit v1 on v0

--- a/solution.py
+++ b/solution.py
@@ -95,7 +95,9 @@
 
 
 def project_back(whole_grad, out_weight):
-    whole_rows = lax.all_gather(out_weight, "dp", axis=1, tiled=True)
+    whole_rows = jnp.concatenate(
+        lax.all_to_all(jnp.stack([out_weight] * lax.axis_size("dp")), "dp", 0, 0), axis=1
+    )
     return lax.dot_general(
         whole_grad, whole_rows, (((1,), (1,)), ((), ())), preferred_element_type=jnp.float32
     )

time: 642 us -> 584 us (0.910)
  waiting for transfers between devices: 409 us -> 315 us
  blocking collectives: 0 us -> 20.6 us
  starting transfers between devices: 29.9 us -> 43.9 us
    all_gather x1, waiting for transfers between devices: 93.7 us -> 0.01 us  [per_device(): whole_grad = lax.all_gather(grad_out, 'seq', axis=0, tiled=True)]
    all_to_all x1, waiting for transfers between devices: 8.29 us -> 89.8 us  [project_back(): lax.all_to_all(jnp.stack([out_weight] * lax.axis_size('dp')), 'dp', 0, 0)]
    all_gather x1 -> x0, waiting for transfers between devices: 70.3 us -> none  [project_back(): whole_rows = lax.all_gather(out_weight, 'dp', axis=1, tiled=True)]
    all_to_all x0 -> x1, blocking collectives: none -> 20.6 us  [per_device(): lax.all_to_all(value_states, 'seq', split_axis=1, concat_axis=0, tiled=True)]
    all_to_all x1, starting transfers between devices: 4.9 us -> 18.9 us  [project_back(): lax.all_to_all(jnp.stack([out_weight] * lax.axis_size('dp')), 'dp', 0, 0)]
    unnamed x4 -> x3, waiting for transfers between devices: 194 us -> 187 us
  transfers between devices with their start and end apart: 8 -> 7, of which waited for: 8 -> 6; matrix products, arithmetic and copies ran while one was open for 2% -> 2% of each run, Pallas kernels for 0% -> 0%
where the time goes in v1:
time: 584 us; the launch traced here: 582 us
  waiting for transfers between devices  315 us (54%)
  matrix products  126 us (22%)
  local copies, waits for them, and re-layouts  56 us (10%)
  starting transfers between devices  43.9 us (8%)
  blocking collectives  20.6 us (4%)
  between operations  14.2 us (2%)
  other arithmetic  5.88 us (1%)
    unnamed x3, waiting for transfers between devices  187 us
    all_to_all x1, waiting for transfers between devices, project_back(): lax.all_to_all(jnp.stack([out_weight] * lax.axis_size('dp')), 'dp', 0, 0)  89.8 us
    dot_general x6, matrix products, backward_rows(): jnp.einsum('rqk,rqd->rkd', dscore, query_rows, preferred_element_type=jnp...  39.7 us
    dot_general x6, matrix products, backward_rows(): jnp.einsum('rqk,rkd->rqd', dscore, key_rows, preferred_element_type=jnp.f...  27.4 us
    all_to_all x1, blocking collectives, per_device(): lax.all_to_all(value_states, 'seq', split_axis=1, concat_axis=0, tiled=True)  20.6 us
    all_to_all x1, starting transfers between devices, project_back(): lax.all_to_all(jnp.stack([out_weight] * lax.axis_size('dp')), 'dp', 0, 0)  18.9 us
    dot_general x3, matrix products, attend_full(): jnp.einsum('msn,msbd->nbd', spread, mid_dk.reshape(chosen.shape[0], slot_...  18.3 us
    dot_general x6, matrix products, forward_rows(): jnp.einsum('rqk,rkd->rqd', probs.astype(jnp.bfloat16), value_rows, prefer...  12.9 us
  transfers between devices with their start and end apart: 7, of which 6 were waited for; matrix products, arithmetic and copies ran while one was open for 2% of the time, Pallas kernels for 0%

profile of v1, /device:TPU:8, one launch (start us, length us, event | category | flops | bytes accessed | tf_op | source)
XLA Modules:
  0.0 582.1 jit_solution(14631367050300641687)
XLA Ops:
  7.2 2.4 copy.57
  9.6 9.3 %all-to-all-start = ((bf16[128,8,384]{0,2,1:T(8,128)(2,1)}), bf16[128,8,384]{0,2,1:T(8,128)(2,1)S(1)}, u32[]{:S(2)}, u32[]{:S(2)}) async-start(bf16[128,8,384]{0,2,1:T(8,128)(2,1)} %bitcast.19), calls=%async_computation | async-start | bytes 1572864 | tf_op jit(solution)/shard_map/all_to_all | solution.py:119
  19.6 1.2 copy.59
  20.7 7.9 %all-to-all-done = bf16[128,8,384]{0,2,1:T(8,128)(2,1)S(1)} async-done(((bf16[128,8,384]{0,2,1:T(8,128)(2,1)}), bf16[128,8,384]{0,2,1:T(8,128)(2,1)S(1)}, u32[]{:S(2)}, u32[]{:S(2)}) %all-to-all-start) | async-done | bytes 786464 | tf_op jit(solution)/shard_map/all_to_all | solution.py:119
  28.7 5.4 all-to-all-start.1
  34.4 10.7 %all-to-all-done.1 = bf16[128,8,384]{0,2,1:T(8,128)(2,1)S(1)} async-done(((bf16[128,8,384]{0,2,1:T(8,128)(2,1)}), bf16[128,8,384]{0,2,1:T(8,128)(2,1)S(1)}, u32[]{:S(2)}, u32[]{:S(2)}) %all-to-all-start.1) | async-done | bytes 786464 | tf_op jit(solution)/shard_map/all_to_all | solution.py:120
  45.2 20.6 %all_to_all.91 = bf16[128,8,384]{0,2,1:T(8,128)(2,1)S(1)} all-to-all(bf16[128,8,384]{0,2,1:T(8,128)(2,1)S(1)} %bitcast.165), channel_id=1, replica_groups=mesh['dp'=64,'seq'=8] {'seq'}, dimensions={1} | all-to-all | bytes 1572864 | tf_op jit(solution)/shard_map/all_to_all | solution.py:121
  65.8 1.5 stack.6
  67.3 18.9 %all-to-all-start.3 = ((bf16[64,384,40]{1,2,0:T(8,128)(2,1)}), bf16[64,384,40]{1,2,0:T(8,128)(2,1)}, u32[]{:S(2)}, u32[]{:S(2)}) async-start(bf16[64,384,40]{1,2,0:T(8,128)(2,1)} %stack.6), calls=%async_computation.3 | async-start | bytes 3932160 | tf_op jit(solution)/shard_map/all_to_all | solution.py:99
  88.8 1.3 reshape.108
  90.6 1.2 reshape.109
  91.8 89.8 %all-to-all-done.3 = bf16[64,384,40]{1,2,0:T(8,128)(2,1)} async-done(((bf16[64,384,40]{1,2,0:T(8,128)(2,1)}), bf16[64,384,40]{1,2,0:T(8,128)(2,1)}, u32[]{:S(2)}, u32[]{:S(2)}) %all-to-all-start.3) | async-done | bytes 1966112 | tf_op jit(solution)/shard_map/all_to_all | solution.py:99
  181.6 5.3 convolution_convert_fusion.3
  187.0 1.2 copy.65
  188.2 152.2 %while.14 = (s32[]{:T(128)}, bf16[3,1024,128]{2,1,0:T(8,128)(2,1)}, bf16[3,1024,128]{2,1,0:T(8,128)(2,1)}, bf16[3,1024,128]{2,1,0:T(8,128)(2,1)}, bf16[3,1024,12...) while((s32[]{:T(128)}, bf16[3,1024,128]{2,1,0:T(8,128)(2,1)}, ...), condition=%wide.region_7.8_spmd, body=%wide.region_0.7_spmd.sunk | while | flops 979120320 | bytes 70489952 | solution.py:144
  197.4 2.1 gather_fusion.1
  199.5 3.5 fusion.160
  203.8 1.8 fusion.162
  205.6 3.7 convolution_convert_fusion.9
  209.3 8.7 %fusion.163 = bf16[14,64,128]{2,1,0:T(8,128)(2,1)} fusion(bf16[14,512,128]{2,1,0:T(8,128)(2,1)S(1)} %bitcast.148, f32[14,64,512]{2,1,0:T(8,128)} %fusion.160, f32[14,64,512]{2,1,0:T(8,128)} %get-tuple-element.217, f32[14,64]{1,0:T(8,128)S(1)} %get-tuple-element.218), kind=kOutput, calls=%fused_computation.27.clone.1 | convolution fusion | flops 120767872 | bytes 5737984 | tf_op jit(solution)/shard_map/while/body/eval_jaxpr/rqk,rkd->rqd/dot_general | solution.py:31
  218.1 10.8 %fusion.165 = f32[14,512,128]{2,1,0:T(8,128)} fusion(bf16[14,64,128]{2,1,0:T(8,128)(2,1)S(1)} %bitcast.155, f32[14,64,512]{2,1,0:T(8,128)} %fusion.160, f32[14,64,512]{2,1,0:T(8,128)} %get-tuple-element.217, f32[14,64]{1,0:T(8,128)S(1)} %get-tuple-element.218), kind=kOutput, calls=%fused_computation.14.clone.1 | convolution fusion | flops 120653184 | bytes 7572992 | tf_op jit(solution)/shard_map/while/body/eval_jaxpr/rqk,rqd->rkd/dot_general | solution.py:32
  228.9 6.1 %fusion.166 = f32[16,64,128]{2,0,1:T(8,128)S(1)} fusion(f32[14,8,64,128]{3,2,1,0:T(8,128)} %bitcast.151, s32[14,8]{0,1:T(8,128)S(1)} %copy.107), kind=kOutput, calls=%fused_computation.17.clone.1 | convolution fusion | flops 176162560 | bytes 4194752 | tf_op jit(solution)/shard_map/while/body/eval_jaxpr/msn,msbd->nbd/dot_general | solution.py:86
  235.2 2.5 fusion.167
  248.2 2.1 gather_fusion.1
  250.3 3.5 fusion.160
  254.5 1.8 fusion.162
  256.3 3.7 convolution_convert_fusion.9
  260.1 8.7 %fusion.163 = bf16[14,64,128]{2,1,0:T(8,128)(2,1)} fusion(bf16[14,512,128]{2,1,0:T(8,128)(2,1)S(1)} %bitcast.148, f32[14,64,512]{2,1,0:T(8,128)} %fusion.160, f32[14,64,512]{2,1,0:T(8,128)} %get-tuple-element.217, f32[14,64]{1,0:T(8,128)S(1)} %get-tuple-element.218), kind=kOutput, calls=%fused_computation.27.clone.1 | convolution fusion | flops 120767872 | bytes 5737984 | tf_op jit(solution)/shard_map/while/body/eval_jaxpr/rqk,rkd->rqd/dot_general | solution.py:31
  268.8 10.8 %fusion.165 = f32[14,512,128]{2,1,0:T(8,128)} fusion(bf16[14,64,128]{2,1,0:T(8,128)(2,1)S(1)} %bitcast.155, f32[14,64,512]{2,1,0:T(8,128)} %fusion.160, f32[14,64,512]{2,1,0:T(8,128)} %get-tuple-element.217, f32[14,64]{1,0:T(8,128)S(1)} %get-tuple-element.218), kind=kOutput, calls=%fused_computation.14.clone.1 | convolution fusion | flops 120653184 | bytes 7572992 | tf_op jit(solution)/shard_map/while/body/eval_jaxpr/rqk,rqd->rkd/dot_general | solution.py:32
  279.6 6.1 %fusion.166 = f32[16,64,128]{2,0,1:T(8,128)S(1)} fusion(f32[14,8,64,128]{3,2,1,0:T(8,128)} %bitcast.151, s32[14,8]{0,1:T(8,128)S(1)} %copy.107), kind=kOutput, calls=%fused_computation.17.clone.1 | convolution fusion | flops 176162560 | bytes 4194752 | tf_op jit(solution)/shard_map/while/body/eval_jaxpr/msn,msbd->nbd/dot_general | solution.py:86
  285.9 2.4 fusion.167
  298.9 2.1 gather_fusion.1
  301.0 3.5 fusion.160
  305.3 1.8 fusion.162
  307.1 3.7 convolution_convert_fusion.9
  310.8 8.7 %fusion.163 = bf16[14,64,128]{2,1,0:T(8,128)(2,1)} fusion(bf16[14,512,128]{2,1,0:T(8,128)(2,1)S(1)} %bitcast.148, f32[14,64,512]{2,1,0:T(8,128)} %fusion.160, f32[14,64,512]{2,1,0:T(8,128)} %get-tuple-element.217, f32[14,64]{1,0:T(8,128)S(1)} %get-tuple-element.218), kind=kOutput, calls=%fused_computation.27.clone.1 | convolution fusion | flops 120767872 | bytes 5737984 | tf_op jit(solution)/shard_map/while/body/eval_jaxpr/rqk,rkd->rqd/dot_general | solution.py:31
  319.5 10.8 %fusion.165 = f32[14,512,128]{2,1,0:T(8,128)} fusion(bf16[14,64,128]{2,1,0:T(8,128)(2,1)S(1)} %bitcast.155, f32[14,64,512]{2,1,0:T(8,128)} %fusion.160, f32[14,64,512]{2,1,0:T(8,128)} %get-tuple-element.217, f32[14,64]{1,0:T(8,128)S(1)} %get-tuple-element.218), kind=kOutput, calls=%fused_computation.14.clone.1 | convolution fusion | flops 120653184 | bytes 7572992 | tf_op jit(solution)/shard_map/while/body/eval_jaxpr/rqk,rqd->rkd/dot_general | solution.py:32
  330.3 6.1 %fusion.166 = f32[16,64,128]{2,0,1:T(8,128)S(1)} fusion(f32[14,8,64,128]{3,2,1,0:T(8,128)} %bitcast.151, s32[14,8]{0,1:T(8,128)S(1)} %copy.107), kind=kOutput, calls=%fused_computation.17.clone.1 | convolution fusion | flops 176162560 | bytes 4194752 | tf_op jit(solution)/shard_map/while/body/eval_jaxpr/msn,msbd->nbd/dot_general | solution.py:86
  336.6 2.4 fusion.167
  340.4 6.9 %fusion.81 = f32[3,128,2560]{2,1,0:T(8,128)} fusion(bf16[3,1024,128]{2,1,0:T(8,128)(2,1)} %get-tuple-element.59, bf16[1024,2560]{1,0:T(8,128)(2,1)} %all-gather.2.cloned.1.call-done), kind=kOutput, calls=%fused_computation.93 | convolution fusion | flops 2013265920 | bytes 9961472 | tf_op jit(solution)/shard_map/hld,lc->hdc/dot_general | solution.py:108
  347.3 5.5 copy.74
  355.4 5.5 all-to-all-start.5
  362.3 10.7 %all-to-all-done.5 = bf16[8,128,384]{1,2,0:T(8,128)(2,1)S(1)} async-done(((bf16[8,128,384]{1,2,0:T(8,128)(2,1)}), bf16[8,128,384]{1,2,0:T(8,128)(2,1)S(1)}, u32[]{:S(2)}, u32[]{:S(2)}) %all-to-all-start.5) | async-done | bytes 786464 | tf_op jit(solution)/shard_map/all_to_all | solution.py:148
  373.0 4.8 all-to-all-start.4
  377.8 1.2 copy.76
  379.0 9.2 %all-to-all-done.4 = bf16[8,128,384]{1,2,0:T(8,128)(2,1)S(1)} async-done(((bf16[8,128,384]{1,2,0:T(8,128)(2,1)}), bf16[8,128,384]{1,2,0:T(8,128)(2,1)S(1)}, u32[]{:S(2)}, u32[]{:S(2)}) %all-to-all-start.4) | async-done | bytes 786464 | tf_op jit(solution)/shard_map/all_to_all | solution.py:147
  388.1 1.2 copy.75
  389.3 185.9 %reduce-scatter.5.cloned.1.call-done = f32[384,40]{0,1:T(8,128)} async-done(((f32[384,2560]{0,1:T(8,128)}), f32[384,40]{0,1:T(8,128)}) %reduce-scatter.5.cloned.1.call-update) | async-done | bytes 61456
  (202 shorter events, 42.1 us)
Async XLA Ops:
  7.2 79.4 %copy-start = (s32[24,16,16]{0,2,1:T(8,128)S(1)}, s32[24,16,16]{0,2,1:T(8,128)}, u32[]{:S(2)}) copy-start(s32[24,16,16]{0,2,1:T(8,128)} %param.14) | copy-start | bytes 73732
  7.2 12.4 %copy-start.8 = (bf16[128,3072]{1,0:T(8,128)(2,1)S(1)}, bf16[128,3072]{1,0:T(8,128)(2,1)}, u32[]{:S(2)}) copy-start(bf16[128,3072]{1,0:T(8,128)(2,1)} %param.10) | copy-start | bytes 2359300
  9.6 19.1 %all-to-all-start = ((bf16[128,8,384]{0,2,1:T(8,128)(2,1)}), bf16[128,8,384]{0,2,1:T(8,128)(2,1)S(1)}, u32[]{:S(2)}, u32[]{:S(2)}) async-start(bf16[128,8,384]{0,2,1:T(8,128)(2,1)} %bitcast.19), calls=%async_computation | async-start | bytes 1572864 | tf_op jit(solution)/shard_map/all_to_all | solution.py:119
  18.8 15.2 %copy-start.9 = (bf16[128,3072]{1,0:T(8,128)(2,1)S(1)}, bf16[128,3072]{1,0:T(8,128)(2,1)}, u32[]{:S(2)}) copy-start(bf16[128,3072]{1,0:T(8,128)(2,1)} %param.11) | copy-start | bytes 2359300
  18.8 162.8 %all-gather.2.cloned.1.call-start = ((), (), s32[]{:S(2)}) async-start(), calls=%async_computation.7 | async-start | bytes 5898240 | tf_op jit(solution)/shard_map/all_gather | solution.py:123
  28.7 16.5 %all-to-all-start.1 = ((bf16[128,8,384]{0,2,1:T(8,128)(2,1)}), bf16[128,8,384]{0,2,1:T(8,128)(2,1)S(1)}, u32[]{:S(2)}, u32[]{:S(2)}) async-start(bf16[128,8,384]{0,2,1:T(8,128)(2,1)} %bitcast.22), calls=%async_computation.1 | async-start | bytes 1572864 | tf_op jit(solution)/shard_map/all_to_all | solution.py:120
  34.1 31.8 %copy-start.12 = (bf16[384,40]{0,1:T(8,128)(2,1)S(1)}, bf16[384,40]{0,1:T(8,128)(2,1)}, u32[]{:S(2)}) copy-start(bf16[384,40]{0,1:T(8,128)(2,1)} %param.13) | copy-start | bytes 92164
  67.3 19.0 %copy-start.15 = (s32[24,16]{0,1:T(8,128)S(1)}, s32[24,16]{0,1:T(8,128)}, u32[]{:S(2)}) copy-start(s32[24,16]{0,1:T(8,128)} %param.15) | copy-start | bytes 4612
  67.3 114.3 %all-to-all-start.3 = ((bf16[64,384,40]{1,2,0:T(8,128)(2,1)}), bf16[64,384,40]{1,2,0:T(8,128)(2,1)}, u32[]{:S(2)}, u32[]{:S(2)}) async-start(bf16[64,384,40]{1,2,0:T(8,128)(2,1)} %stack.6), calls=%async_computation.3 | async-start | bytes 3932160 | tf_op jit(solution)/shard_map/all_to_all | solution.py:99
  86.3 488.9 %reduce-scatter.5.cloned.1.call-start = ((), (), s32[]{:S(2)}) async-start(), calls=%async_computation.8 | async-start | bytes 3993600
  188.2 2.1 copy-start.16
  188.2 3.6 copy-start.3
  194.4 0.9 copy-start.2
  194.9 1.0 copy-start.13
  203.8 1.8 copy-start.1
  228.8 6.3 %copy-start.14 = (f32[2,64]{1,0:T(2,128)S(1)}, f32[2,64]{1,0:T(2,128)}, u32[]{:S(2)}) copy-start(f32[2,64]{1,0:T(2,128)} %copy-done.13) | copy-start | bytes 1540 | tf_op jit(solution)/shard_map/while
  234.9 2.7 copy-start.5
  235.1 2.5 copy-start.6
  235.1 2.5 copy-start.7
  237.6 1.3 copy-start.4
  237.6 1.3 copy-start.17
  238.9 2.1 copy-start.16
  238.9 3.6 copy-start.3
  245.2 0.9 copy-start.2
  245.6 1.0 copy-start.13
  254.5 1.8 copy-start.1
  279.6 6.3 %copy-start.14 = (f32[2,64]{1,0:T(2,128)S(1)}, f32[2,64]{1,0:T(2,128)}, u32[]{:S(2)}) copy-start(f32[2,64]{1,0:T(2,128)} %copy-done.13) | copy-start | bytes 1540 | tf_op jit(solution)/shard_map/while
  285.7 2.7 copy-start.5
  285.9 2.5 copy-start.6
  285.9 2.5 copy-start.7
  288.4 1.3 copy-start.4
  288.4 1.3 copy-start.17
  289.7 2.1 copy-start.16
  289.7 3.6 copy-start.3
  295.9 0.9 copy-start.2
  296.4 1.0 copy-start.13
  305.3 1.8 copy-start.1
  330.3 6.3 %copy-start.14 = (f32[2,64]{1,0:T(2,128)S(1)}, f32[2,64]{1,0:T(2,128)}, u32[]{:S(2)}) copy-start(f32[2,64]{1,0:T(2,128)} %copy-done.13) | copy-start | bytes 1540 | tf_op jit(solution)/shard_map/while
  336.4 2.7 copy-start.5
  336.6 2.5 copy-start.6
  336.6 2.5 copy-start.7
  339.1 1.3 copy-start.4
  339.1 1.3 copy-start.17
  352.8 1.1 copy-start.10
  354.4 6.5 %copy-start.11 = (bf16[3,1024,128]{2,1,0:T(8,128)(2,1)S(1)}, bf16[3,1024,128]{2,1,0:T(8,128)(2,1)}, u32[]{:S(2)}) copy-start(bf16[3,1024,128]{2,1,0:T(8,128)(2,1)} %get-tuple-element.57) | copy-start | bytes 2359300
  355.4 17.6 %all-to-all-start.5 = ((bf16[8,128,384]{1,2,0:T(8,128)(2,1)}), bf16[8,128,384]{1,2,0:T(8,128)(2,1)S(1)}, u32[]{:S(2)}, u32[]{:S(2)}) async-start(bf16[8,128,384]{1,2,0:T(8,128)(2,1)} %copy.72), calls=%async_computation.5 | async-start | bytes 1572864 | tf_op jit(solution)/shard_map/all_to_all | solution.py:148
  373.0 15.1 %all-to-all-start.4 = ((bf16[8,128,384]{1,2,0:T(8,128)(2,1)}), bf16[8,128,384]{1,2,0:T(8,128)(2,1)S(1)}, u32[]{:S(2)}, u32[]{:S(2)}) async-start(bf16[8,128,384]{1,2,0:T(8,128)(2,1)} %copy.70), calls=%async_computation.4 | async-start | bytes 1572864 | tf_op jit(solution)/shard_map/all_to_all | solution.py:147
Sparse Core Ops, SparseCore 0:
  22.8 113.4 all-gather.1
  352.9 222.2 reduce-scatter.4
